TPU v7x, 256 devices: a whole 4x4x8 slice. The times are simulated.
256 devices in a mesh: dp: 4 (over x), expert: 32 (over z, y), tensor: 2 (over core).
Axes of the slice: x: 4, y: 4, z: 8, core: 2. Of those that a mesh axis runs over, the one named last changes fastest.
Arguments:
- queries: bfloat16 [8192, 4096], P(('dp', 'expert'), 'tensor'), may hold values from -8 to 8
- fresh_keys: bfloat16 [8192, 512], P(('dp', 'expert'), 'tensor'), may hold values from -6 to 6
- fresh_values: bfloat16 [8192, 512], P(('dp', 'expert'), 'tensor'), may hold values from -6 to 6
- resident_keys: bfloat16 [128, 2048, 512], P(('dp', 'expert'), None, 'tensor'), may hold values from -8 to 8
- resident_values: bfloat16 [128, 2048, 512], P(('dp', 'expert'), None, 'tensor'), may hold values from -6 to 6
- out_weight: bfloat16 [4096, 2048], P('tensor', 'dp'), may hold values from -0.5 to 0.5
- residual: bfloat16 [8192, 2048], P(('dp', 'expert')), may hold values from -23 to 23
- norm_gain: float32 [2048], replicated, may hold values from 0.1 to 1.9
- expert_ids: int32 [8192, 8], P(('dp', 'expert')), may hold values from 0 to 127, all different within a row; in each aligned block of 64 rows (0 to 63, 64 to 127, ...) at most 6 rows name the same one
- gates: float32 [8192, 8], P(('dp', 'expert')), may hold values from 0.05 to 0.5
- w_gate: bfloat16 [128, 2048, 768], P(('dp', 'expert'), None, 'tensor'), may hold values from -0.125 to 0.125
- w_up: bfloat16 [128, 2048, 768], P(('dp', 'expert'), None, 'tensor'), may hold values from -0.125 to 0.125
- w_down: bfloat16 [128, 768, 2048], P(('dp', 'expert'), 'tensor'), may hold values from -0.21875 to 0.21875
Outputs:
- mixed: bfloat16 [8192, 2048], P(('dp', 'expert'), 'tensor')
Inputs may be any that keep to these rules, and one draw needn't show every extreme that they name: `expert_ids`: within the 64 tokens of one sequence no expert is named by more than 6 tokens, a bound that some block reaches; a token names 8 different experts.
All inputs are finite; a program needn't handle non-finite values.
Results may differ from a plain program's by a relative error of at most 0.0085.
Values may be sent and summed in bfloat16 or wider, within the bound.
No kernel may reach another device: no remote copies, remote signals or barrier semaphores. Data moves between devices by JAX's collectives and lax.ppermute only.
A program may use at most 64 MiB of HBM per device.

v0:
```python
import jax
import jax.numpy as jnp
from jax import lax
from jax.sharding import PartitionSpec as P

D = 2048
HEAD_WIDTH = 128


def attend_local(queries, fresh_keys, fresh_values, resident_keys, resident_values):
    tokens_here = queries.shape[0]
    kv_here = fresh_keys.shape[1] // HEAD_WIDTH
    query_group = queries.shape[1] // HEAD_WIDTH // kv_here
    context = resident_keys.shape[1]
    query_rows = queries.reshape(tokens_here, kv_here, query_group, HEAD_WIDTH)
    joined_keys = jnp.concatenate([resident_keys[0], fresh_keys], 0).reshape(
        context + tokens_here, kv_here, HEAD_WIDTH
    )
    joined_values = jnp.concatenate([resident_values[0], fresh_values], 0).reshape(
        context + tokens_here, kv_here, HEAD_WIDTH
    )
    score = jnp.einsum(
        "tjgd,sjd->jgts", query_rows, joined_keys, preferred_element_type=jnp.float32
    ) * HEAD_WIDTH ** (-0.5)
    places = jnp.arange(context + tokens_here)
    rows = jnp.arange(tokens_here)
    allowed = (places[None, :] < context) | (places[None, :] - context <= rows[:, None])
    score = jnp.where(allowed, score, jnp.float32(-1e30))
    top_score = jnp.max(score, axis=-1, keepdims=True)
    weight = jnp.exp(score - top_score)
    probs = (weight / jnp.sum(weight, axis=-1, keepdims=True)).astype(jnp.bfloat16)
    attended = jnp.einsum(
        "jgts,sjd->tjgd", probs, joined_values, preferred_element_type=jnp.float32
    )
    return attended.reshape(tokens_here, -1).astype(jnp.bfloat16)


def expert_rows(block, gate_mat, up_mat, down_mat):
    sources, items, width = block.shape
    flat = block.reshape(sources * items, width)
    gate_part = jnp.dot(flat, gate_mat, preferred_element_type=jnp.float32)
    up_part = jnp.dot(flat, up_mat, preferred_element_type=jnp.float32)
    act = (jax.nn.silu(gate_part) * up_part).astype(jnp.bfloat16)
    result = jnp.dot(act, down_mat, preferred_element_type=jnp.float32)
    return result.reshape(sources, items, -1)


def per_device(
    queries,
    fresh_keys,
    fresh_values,
    resident_keys,
    resident_values,
    out_weight,
    residual,
    norm_gain,
    expert_ids,
    gates,
    w_gate,
    w_up,
    w_down,
):
    attended = attend_local(queries, fresh_keys, fresh_values, resident_keys, resident_values)
    partial_sum = jnp.dot(
        attended,
        lax.all_gather(out_weight, "dp", axis=1, tiled=True),
        preferred_element_type=jnp.float32,
    )
    tokens_here = residual.shape[0]
    pairs = lax.axis_size("tensor")
    half = D // pairs
    lane = lax.axis_index("tensor")
    summed = lax.psum(partial_sum.astype(jnp.bfloat16), "tensor").astype(jnp.float32)
    hidden = residual.astype(jnp.float32) + summed
    mean_square = jnp.mean(hidden * hidden, axis=-1, keepdims=True)
    normed = (hidden * lax.rsqrt(mean_square + 1e-06) * norm_gain).astype(jnp.bfloat16)
    hidden_half = lax.dynamic_slice_in_dim(hidden, lane * half, half, 1)
    owners = lax.axis_size("dp") * lax.axis_size("expert")
    top = expert_ids.shape[1]
    slots = max(2, tokens_here * top * 3 // (2 * owners))
    onehot = (expert_ids[:, :, None] == jnp.arange(owners)[None, None, :]).astype(jnp.int32)
    per_token = jnp.sum(onehot, axis=1)
    before = jnp.cumsum(per_token, axis=0) - per_token
    slot = jnp.sum(onehot * before[:, None, :], axis=-1)
    token_rows = jnp.broadcast_to(
        jnp.arange(tokens_here, dtype=jnp.int32)[:, None], expert_ids.shape
    )
    owner_rows = jnp.full((owners, slots), -1, jnp.int32).at[expert_ids, slot].set(token_rows)
    valid = owner_rows >= 0
    outgoing = jnp.where(
        valid[:, :, None], normed[jnp.maximum(owner_rows, 0)], jnp.zeros((), jnp.bfloat16)
    )
    expert_part = expert_rows(
        lax.all_to_all(outgoing, ("dp", "expert"), split_axis=0, concat_axis=0, tiled=True),
        w_gate[0],
        w_up[0],
        w_down[0],
    )
    owned = lax.psum_scatter(
        expert_part.astype(jnp.bfloat16), "tensor", scatter_dimension=2, tiled=True
    )
    returned = lax.all_to_all(owned, ("dp", "expert"), split_axis=0, concat_axis=0, tiled=True)
    picked = returned[expert_ids, slot]
    moe = jnp.sum(gates[:, :, None] * picked.astype(jnp.float32), axis=1)
    return (hidden_half + moe).astype(jnp.bfloat16)


def solution(mesh):
    return jax.shard_map(
        per_device,
        mesh=mesh,
        in_specs=(
            P(("dp", "expert"), "tensor"),
            P(("dp", "expert"), "tensor"),
            P(("dp", "expert"), "tensor"),
            P(("dp", "expert"), None, "tensor"),
            P(("dp", "expert"), None, "tensor"),
            P("tensor", "dp"),
            P(("dp", "expert"), None),
            P(),
            P(("dp", "expert"), None),
            P(("dp", "expert"), None),
            P(("dp", "expert"), None, "tensor"),
            P(("dp", "expert"), None, "tensor"),
            P(("dp", "expert"), "tensor", None),
        ),
        out_specs=P(("dp", "expert"), "tensor"),
        check_vma=False,
    )
```

profile of v0, /device:TPU:32, one launch (start us, length us, event | category | flops | bytes accessed | tf_op | source)
XLA Modules:
  0.0 379.2 jit_solution(17011101792321861209)
XLA Ops:
  6.5 0.7 all-gather.2.cloned.1.call-update
  7.3 1.5 copy.74
  8.8 1.4 copy.75
  10.3 1.5 copy.71
  11.8 1.3 copy.72
  13.3 4.6 %fusion.46 = f32[2,8,64]{2,1,0:T(8,128)S(1)} fusion(pred[64,2112]{1,0:T(8,128)(4,1)S(1)} %fusion.26, bf16[64,2,128]{2,0,1:T(8,128)(2,1)S(1)} %get-tuple-element.9, bf16[2048,2,128]{2,0,1:T(8,128)(2,1)} %copy.75, bf16[64,2,8,128]{3,2,1,0:T(8,128)(2,1)S(1)} %bitcast.97), kind=kOutput, calls=%fused_computation.69 | convolution fusion | flops 564463680 | bytes 1482752 | tf_op jit(solution)/shard_map/sub | solution.py:30
  17.9 4.9 %fusion.19 = bf16[64,2,8,128]{3,0,2,1:T(8,128)(2,1)S(1)} fusion(f32[2,8,64]{2,1,0:T(8,128)S(1)} %fusion.46, bf16[64,2,128]{2,0,1:T(8,128)(2,1)S(1)} %get-tuple-element.10, bf16[2048,2,128]{2,0,1:T(8,128)(2,1)} %copy.72, pred[64,2112]{1,0:T(8,128)(4,1)S(1)} %fusion.26, bf16[64,2,128]{2,0,1:T(8,128)(2,1)S(1)} %get-tuple-element.9, ...), kind=kOutput, calls=%fused_computation.25 | convolution fusion | flops 1122569216 | bytes 2826240 | tf_op jit(solution)/shard_map/jgts,sjd->tjgd/dot_general | solution.py:32
  23.4 1.2 select_reduce_fusion
  25.0 22.0 %scatter_fusion = s32[128,6]{0,1:T(8,128)S(1)} fusion(s32[128,6]{0,1:T(8,128)S(1)} %broadcast_in_dim.26, s32[512]{0:T(512)S(1)} %reshape.80, s32[512]{0:T(512)S(1)} %reshape.82), kind=kCustom, calls=%fused_computation.2 | custom fusion | bytes 10240 | tf_op jit(solution)/shard_map/scatter | solution.py:88
  47.3 50.1 %all-gather.2.cloned.1.call-done = bf16[2048,2048]{1,0:T(8,128)(2,1)} async-done(((bf16[2048,512]{1,0:T(8,128)(2,1)}), bf16[2048,2048]{1,0:T(8,128)(2,1)}) %all-gather.2.cloned.1.call-update) | async-done | bytes 8388624 | tf_op jit(solution)/shard_map/all_gather | solution.py:66
  97.4 5.7 %convolution_convert_fusion.1 = bf16[64,2048]{1,0:T(8,128)(2,1)} fusion(bf16[2048,2048]{1,0:T(8,128)(2,1)} %all-gather.2.cloned.1.call-done, bf16[8,8,16,128]{3,2,1,0:T(8,128)(2,1)S(1)} %bitcast.95), kind=kOutput, calls=%fused_computation.14 | convolution fusion | flops 537001984 | bytes 8912896 | tf_op jit(solution)/shard_map/dot_general | solution.py:64
  103.1 0.2 reduce-scatter.2.cloned.1.call-start
  103.5 29.8 %all-reduce.2.cloned.1.call-done = bf16[64,2048]{1,0:T(8,128)(2,1)} async-done(((bf16[64,2048]{1,0:T(8,128)(2,1)}), bf16[64,2048]{1,0:T(8,128)(2,1)}) %all-reduce.2.cloned.1.call-update) | async-done | bytes 262160 | tf_op jit(solution)/shard_map/psum | solution.py:73
  133.3 1.9 convert_add_fusion
  135.3 1.1 multiply_convert_fusion
  136.3 4.3 %gather_fusion = bf16[768,2048]{1,0:T(8,128)(2,1)} fusion(bf16[64,2048]{1,0:T(8,128)(2,1)S(1)} %multiply_convert_fusion, s32[1024]{0:T(1024)S(1)} %pad_clamp_fusion), kind=kCustom, calls=%fused_computation | custom fusion | bytes 6294528 | tf_op jit(solution)/shard_map/gather | solution.py:91
  140.6 6.3 %reshape.67 = bf16[128,6,2048]{2,1,0:T(8,128)(2,1)} reshape(bf16[768,2048]{1,0:T(8,128)(2,1)} %gather_fusion) | data formatting | bytes 6291456 | tf_op jit(solution)/shard_map/gather | solution.py:91
  146.9 2.6 broadcast_select_fusion
  149.5 111.2 %all_to_all.10 = bf16[128,6,2048]{2,1,0:T(8,128)(2,1)} all-to-all(bf16[128,6,2048]{2,1,0:T(8,128)(2,1)S(1)} %broadcast_select_fusion), channel_id=1, replica_groups=mesh['dp'=4,'expert'=32,'tensor'=2] {'dp','expert'}, dimensions={0} | all-to-all | bytes 6291456 | tf_op jit(solution)/shard_map/all_to_all | solution.py:94
  260.8 6.3 %reshape.65 = bf16[768,2048]{1,0:T(8,128)(2,1)} reshape(bf16[128,6,2048]{2,1,0:T(8,128)(2,1)} %all_to_all.10) | data formatting | bytes 6291456 | tf_op jit(solution)/shard_map/reshape | solution.py:40
  267.1 4.3 %fusion.10 = f32[768,384]{1,0:T(8,128)S(1)} fusion(bf16[768,2048]{1,0:T(8,128)(2,1)} %reshape.65, bf16[1,2048,384]{2,1,0:T(8,128)(2,1)} %param.23), kind=kOutput, calls=%fused_computation.20 | convolution fusion | flops 1207959552 | bytes 5898240 | tf_op jit(solution)/shard_map/dot_general | solution.py:41
  271.4 1.8 fusion.15
  273.3 0.2 dot_general.25
  273.5 3.5 convolution_convert_fusion
  277.0 11.5 %reduce-scatter.2.cloned.1.call-done = bf16[128,6,1024]{2,0,1:T(8,128)(2,1)} async-done(((bf16[128,6,2048]{2,0,1:T(8,128)(2,1)}), bf16[128,6,1024]{2,0,1:T(8,128)(2,1)}) %reduce-scatter.2.cloned.1.call-update) | async-done | bytes 1572880 | tf_op jit(solution)/shard_map/reduce_scatter | solution.py:99
  288.4 3.6 copy.86
  292.1 14.3 %all-to-all-start.1 = ((bf16[128,6,1024]{2,1,0:T(8,128)(2,1)}), bf16[128,6,1024]{2,1,0:T(8,128)(2,1)}, u32[]{:S(2)}, u32[]{:S(2)}) async-start(bf16[128,6,1024]{2,1,0:T(8,128)(2,1)} %copy.86), calls=%async_computation.2 | async-start | bytes 4194304 | tf_op jit(solution)/shard_map/all_to_all | solution.py:102
  306.7 52.1 %all-to-all-done.1 = bf16[128,6,1024]{2,1,0:T(8,128)(2,1)} async-done(((bf16[128,6,1024]{2,1,0:T(8,128)(2,1)}), bf16[128,6,1024]{2,1,0:T(8,128)(2,1)}, u32[]{:S(2)}, u32[]{:S(2)}) %all-to-all-start.1) | async-done | bytes 1572896 | tf_op jit(solution)/shard_map/all_to_all | solution.py:102
  358.8 2.5 copy.88
  361.2 7.9 %gather_fusion.1 = bf16[512,1024]{1,0:T(8,128)(2,1)} fusion(bf16[128,6,1024]{2,0,1:T(8,128)(2,1)S(1)} %copy.88, s32[512]{0:T(512)S(1)} %reshape.74), kind=kCustom, calls=%fused_computation.1 | custom fusion | bytes 2101248 | tf_op jit(solution)/shard_map/gather | solution.py:103
  369.1 1.9 fusion.6
  371.0 1.6 add_convert_fusion
  (53 shorter events, 1.8 us)
Async XLA Ops:
  6.5 266.9 %copy-start = (bf16[1,384,2048]{2,1,0:T(8,128)(2,1)S(1)}, bf16[1,384,2048]{2,1,0:T(8,128)(2,1)}, u32[]{:S(2)}) copy-start(bf16[1,384,2048]{2,1,0:T(8,128)(2,1)} %param.25) | copy-start | bytes 4718596
  6.5 90.8 %all-gather.2.cloned.1.call-start = ((), (), s32[]{:S(2)}) async-start(), calls=%async_computation.3 | async-start | bytes 10485760 | tf_op jit(solution)/shard_map/all_gather | solution.py:66
  7.3 3.0 copy-start.4
  7.3 126.1 %all-reduce.2.cloned.1.call-start = ((), (), s32[]{:S(2)}) async-start(), calls=%async_computation.4 | async-start | bytes 524288 | tf_op jit(solution)/shard_map/psum | solution.py:73
  10.3 2.8 copy-start.5
  10.3 2.8 copy-start.6
  13.3 4.7 %copy-start.2 = (bf16[2048,2,128]{2,0,1:T(8,128)(2,1)S(1)}, bf16[2048,2,128]{2,0,1:T(8,128)(2,1)}, u32[]{:S(2)}) copy-start(bf16[2048,2,128]{2,0,1:T(8,128)(2,1)} %copy.75) | copy-start | bytes 3145732
  17.9 5.1 %copy-start.7 = (s32[64,8]{0,1:T(8,128)S(1)}, s32[64,8]{0,1:T(8,128)}, u32[]{:S(2)}) copy-start(s32[64,8]{0,1:T(8,128)} %param.21) | copy-start | bytes 6148
  97.4 35.9 %copy-start.3 = (bf16[64,2048]{1,0:T(8,128)(2,1)S(1)}, bf16[64,2048]{1,0:T(8,128)(2,1)}, u32[]{:S(2)}) copy-start(bf16[64,2048]{1,0:T(8,128)(2,1)} %param.19) | copy-start | bytes 786436
  97.4 37.9 %copy-start.8 = (f32[2048]{0:T(1024)S(1)}, f32[2048]{0:T(1024)}, u32[]{:S(2)}) copy-start(f32[2048]{0:T(1024)} %param.20) | copy-start | bytes 24580
  103.1 185.3 %reduce-scatter.2.cloned.1.call-start = ((), (), s32[]{:S(2)}) async-start(), calls=%async_computation.5 | async-start | bytes 4718592 | tf_op jit(solution)/shard_map/reduce_scatter | solution.py:99
  267.1 4.3 %copy-start.1 = (bf16[768,2048]{1,0:T(8,128)(2,1)S(1)}, bf16[768,2048]{1,0:T(8,128)(2,1)}, u32[]{:S(2)}) copy-start(bf16[768,2048]{1,0:T(8,128)(2,1)} %reshape.65) | copy-start | bytes 9437188
  267.1 4.3 %copy-start.10 = (bf16[1,2048,384]{2,1,0:T(8,128)(2,1)S(1)}, bf16[1,2048,384]{2,1,0:T(8,128)(2,1)}, u32[]{:S(2)}) copy-start(bf16[1,2048,384]{2,1,0:T(8,128)(2,1)} %param.24) | copy-start | bytes 4718596
  292.1 14.5 %copy-start.9 = (f32[64,8]{0,1:T(8,128)S(1)}, f32[64,8]{0,1:T(8,128)}, u32[]{:S(2)}) copy-start(f32[64,8]{0,1:T(8,128)} %param.22) | copy-start | bytes 6148
  292.1 66.7 %all-to-all-start.1 = ((bf16[128,6,1024]{2,1,0:T(8,128)(2,1)}), bf16[128,6,1024]{2,1,0:T(8,128)(2,1)}, u32[]{:S(2)}, u32[]{:S(2)}) async-start(bf16[128,6,1024]{2,1,0:T(8,128)(2,1)} %copy.86), calls=%async_computation.2 | async-start | bytes 4194304 | tf_op jit(solution)/shard_map/all_to_all | solution.py:102
Sparse Core Ops, SparseCore 0:
  9.1 88.1 all-gather.1
  103.2 30.0 all-reduce.1
  277.1 11.3 reduce-scatter.1
where the time goes:
time: 380 us; the launch traced here: 379 us
  waiting for transfers between devices  144 us (38%)
  blocking collectives  111 us (29%)
  local copies, waits for them, and re-layouts  60 us (16%)
  matrix products  24.9 us (7%)
  starting transfers between devices  14.6 us (4%)
  between operations  13.4 us (4%)
  other arithmetic  10.8 us (3%)
    all_to_all x1, blocking collectives, per_device(): lax.all_to_all(outgoing, ('dp', 'expert'), split_axis=0, concat_axis=0, t...  111 us
    all_to_all x1, waiting for transfers between devices, per_device(): lax.all_to_all(owned, ('dp', 'expert'), split_axis=0, concat_axis=0, tile...  52.1 us
    all_gather x1, waiting for transfers between devices, per_device(): lax.all_gather(out_weight, 'dp', axis=1, tiled=True)  50.1 us
    psum x1, waiting for transfers between devices, per_device(): lax.psum(partial_sum.astype(jnp.bfloat16), 'tensor').astype(jnp.float32)  29.8 us
    scatter x1, local copies, waits for them, and re-layouts, per_device(): jnp.full((owners, slots), -1, jnp.int32).at[expert_ids, slot]  22 us
    all_to_all x1, starting transfers between devices, per_device(): lax.all_to_all(owned, ('dp', 'expert'), split_axis=0, concat_axis=0, tile...  14.3 us
    reduce_scatter x1, waiting for transfers between devices, per_device(): lax.psum_scatter(expert_part.astype(jnp.bfloat16), 'tensor', scatter_dime...  11.5 us
    gather x2, local copies, waits for them, and re-layouts, per_device(): normed[jnp.maximum(owner_rows, 0)]  10.5 us
  transfers between devices with their start and end apart: 4, of which 4 were waited for; matrix products, arithmetic and copies ran while one was open for 11% of the time, Pallas kernels for 0%

commit v1 on v0

--- a/solution.py
+++ b/solution.py
@@ -70,7 +70,9 @@
     pairs = lax.axis_size("tensor")
     half = D // pairs
     lane = lax.axis_index("tensor")
-    summed = lax.psum(partial_sum.astype(jnp.bfloat16), "tensor").astype(jnp.float32)
+    summed = jnp.sum(lax.all_gather(partial_sum.astype(jnp.bfloat16), "tensor"), axis=0).astype(
+        jnp.float32
+    )
     hidden = residual.astype(jnp.float32) + summed
     mean_square = jnp.mean(hidden * hidden, axis=-1, keepdims=True)
     normed = (hidden * lax.rsqrt(mean_square + 1e-06) * norm_gain).astype(jnp.bfloat16)

time: 380 us -> 349 us (0.918)
  waiting for transfers between devices: 144 us -> 114 us
    psum x1 -> x0, waiting for transfers between devices: 29.8 us -> none  [per_device(): lax.psum(partial_sum.astype(jnp.bfloat16), 'tensor').astype(jnp.float32)]
  transfers between devices with their start and end apart: 4 -> 3, of which waited for: 4 -> 3; matrix products, arithmetic and copies ran while one was open for 11% -> 12% of each run, Pallas kernels for 0% -> 0%
where the time goes in v1:
time: 349 us
  waiting for transfers between devices  114 us (33%)
  blocking collectives  113 us (32%)
  local copies, waits for them, and re-layouts  60 us (17%)
  matrix products  24.2 us (7%)
  starting transfers between devices  14.3 us (4%)
  between operations  13.7 us (4%)
  other arithmetic  9.05 us (3%)
    all_to_all x1, blocking collectives, per_device(): lax.all_to_all(outgoing, ('dp', 'expert'), split_axis=0, concat_axis=0, t...  111 us
    all_to_all x1, waiting for transfers between devices, per_device(): lax.all_to_all(owned, ('dp', 'expert'), split_axis=0, concat_axis=0, tile...  52.1 us
    all_gather x1, waiting for transfers between devices, per_device(): lax.all_gather(out_weight, 'dp', axis=1, tiled=True)  50 us
    scatter x1, local copies, waits for them, and re-layouts, per_device(): jnp.full((owners, slots), -1, jnp.int32).at[expert_ids, slot]  22 us
    all_to_all x1, starting transfers between devices, per_device(): lax.all_to_all(owned, ('dp', 'expert'), split_axis=0, concat_axis=0, tile...  14.3 us
    reduce_scatter x1, waiting for transfers between devices, per_device(): lax.psum_scatter(expert_part.astype(jnp.bfloat16), 'tensor', scatter_dime...  11.4 us
    gather x2, local copies, waits for them, and re-layouts, per_device(): normed[jnp.maximum(owner_rows, 0)]  10.5 us
    gather x1, local copies, waits for them, and re-layouts, per_device(): picked = returned[expert_ids, slot]  7.86 us
  transfers between devices with their start and end apart: 3, of which 3 were waited for; matrix products, arithmetic and copies ran while one was open for 12% of the time, Pallas kernels for 0%

profile of v1, /device:TPU:32, one launch (start us, length us, event | category | flops | bytes accessed | tf_op | source)
XLA Modules:
  0.0 348.7 jit_solution(3028531344032417523)
XLA Ops:
  6.5 0.7 all-gather.3.cloned.1.call-update
  7.3 1.5 copy.74
  8.8 1.4 copy.75
  10.3 1.5 copy.71
  11.8 1.3 copy.72
  13.3 4.6 %fusion.46 = f32[2,8,64]{2,1,0:T(8,128)S(1)} fusion(pred[64,2112]{1,0:T(8,128)(4,1)S(1)} %fusion.26, bf16[64,2,128]{2,0,1:T(8,128)(2,1)S(1)} %get-tuple-element.9, bf16[2048,2,128]{2,0,1:T(8,128)(2,1)} %copy.75, bf16[64,2,8,128]{3,2,1,0:T(8,128)(2,1)S(1)} %bitcast.99), kind=kOutput, calls=%fused_computation.69 | convolution fusion | flops 564463680 | bytes 1482752 | tf_op jit(solution)/shard_map/sub | solution.py:30
  17.9 4.9 %fusion.19 = bf16[64,2,8,128]{3,0,2,1:T(8,128)(2,1)S(1)} fusion(f32[2,8,64]{2,1,0:T(8,128)S(1)} %fusion.46, bf16[64,2,128]{2,0,1:T(8,128)(2,1)S(1)} %get-tuple-element.10, bf16[2048,2,128]{2,0,1:T(8,128)(2,1)} %copy.72, pred[64,2112]{1,0:T(8,128)(4,1)S(1)} %fusion.26, bf16[64,2,128]{2,0,1:T(8,128)(2,1)S(1)} %get-tuple-element.9, ...), kind=kOutput, calls=%fused_computation.25 | convolution fusion | flops 1122569216 | bytes 2826240 | tf_op jit(solution)/shard_map/jgts,sjd->tjgd/dot_general | solution.py:32
  22.8 0.2 copy.78
  23.1 0.1 convert_reduce_fusion
  23.4 1.2 select_reduce_fusion
  25.0 22.0 %scatter_fusion = s32[128,6]{0,1:T(8,128)S(1)} fusion(s32[128,6]{0,1:T(8,128)S(1)} %broadcast_in_dim.26, s32[512]{0:T(512)S(1)} %reshape.80, s32[512]{0:T(512)S(1)} %reshape.82), kind=kCustom, calls=%fused_computation.2 | custom fusion | bytes 10240 | tf_op jit(solution)/shard_map/scatter | solution.py:90
  47.4 50.0 %all-gather.3.cloned.1.call-done = bf16[2048,2048]{1,0:T(8,128)(2,1)} async-done(((bf16[2048,512]{1,0:T(8,128)(2,1)}), bf16[2048,2048]{1,0:T(8,128)(2,1)}) %all-gather.3.cloned.1.call-update) | async-done | bytes 8388624 | tf_op jit(solution)/shard_map/all_gather | solution.py:66
  97.4 5.0 %convolution_convert_fusion.1 = bf16[64,2048]{1,0:T(8,128)(2,1)S(1)} fusion(bf16[2048,2048]{1,0:T(8,128)(2,1)} %all-gather.3.cloned.1.call-done, bf16[8,8,16,128]{3,2,1,0:T(8,128)(2,1)S(1)} %bitcast.96), kind=kOutput, calls=%fused_computation.14 | convolution fusion | flops 537001984 | bytes 8912896 | tf_op jit(solution)/shard_map/dot_general | solution.py:64
  102.4 2.4 all-gather
  104.9 1.0 convert_add_fusion
  106.0 4.3 %gather_fusion = bf16[768,2048]{1,0:T(8,128)(2,1)} fusion(bf16[64,2048]{1,0:T(8,128)(2,1)S(1)} %multiply_convert_fusion, s32[1024]{0:T(1024)S(1)} %pad_clamp_fusion), kind=kCustom, calls=%fused_computation | custom fusion | bytes 6294528 | tf_op jit(solution)/shard_map/gather | solution.py:93
  110.3 6.3 %reshape.67 = bf16[128,6,2048]{2,1,0:T(8,128)(2,1)} reshape(bf16[768,2048]{1,0:T(8,128)(2,1)} %gather_fusion) | data formatting | bytes 6291456 | tf_op jit(solution)/shard_map/gather | solution.py:93
  116.5 2.6 broadcast_select_fusion
  119.2 110.9 %all_to_all.10 = bf16[128,6,2048]{2,1,0:T(8,128)(2,1)} all-to-all(bf16[128,6,2048]{2,1,0:T(8,128)(2,1)S(1)} %broadcast_select_fusion), channel_id=1, replica_groups=mesh['dp'=4,'expert'=32,'tensor'=2] {'dp','expert'}, dimensions={0} | all-to-all | bytes 6291456 | tf_op jit(solution)/shard_map/all_to_all | solution.py:96
  230.1 6.3 %reshape.65 = bf16[768,2048]{1,0:T(8,128)(2,1)} reshape(bf16[128,6,2048]{2,1,0:T(8,128)(2,1)} %all_to_all.10) | data formatting | bytes 6291456 | tf_op jit(solution)/shard_map/reshape | solution.py:40
  236.4 4.3 %fusion.10 = f32[768,384]{1,0:T(8,128)S(1)} fusion(bf16[768,2048]{1,0:T(8,128)(2,1)} %reshape.65, bf16[1,2048,384]{2,1,0:T(8,128)(2,1)} %param.23), kind=kOutput, calls=%fused_computation.20 | convolution fusion | flops 1207959552 | bytes 5898240 | tf_op jit(solution)/shard_map/dot_general | solution.py:41
  240.7 1.8 fusion.15
  242.6 0.2 dot_general.25
  242.8 3.5 convolution_convert_fusion
  246.3 11.4 %reduce-scatter.2.cloned.1.call-done = bf16[128,6,1024]{2,0,1:T(8,128)(2,1)} async-done(((bf16[128,6,2048]{2,0,1:T(8,128)(2,1)}), bf16[128,6,1024]{2,0,1:T(8,128)(2,1)}) %reduce-scatter.2.cloned.1.call-update) | async-done | bytes 1572880 | tf_op jit(solution)/shard_map/reduce_scatter | solution.py:101
  257.7 3.6 %copy.86 = bf16[128,6,1024]{2,1,0:T(8,128)(2,1)} copy(bf16[128,6,1024]{2,0,1:T(8,128)(2,1)} %reduce-scatter.2.cloned.1.call-done) | data formatting | bytes 3145728 | tf_op jit(solution)/shard_map/reduce_scatter | solution.py:101
  261.3 14.3 %all-to-all-start.1 = ((bf16[128,6,1024]{2,1,0:T(8,128)(2,1)}), bf16[128,6,1024]{2,1,0:T(8,128)(2,1)}, u32[]{:S(2)}, u32[]{:S(2)}) async-start(bf16[128,6,1024]{2,1,0:T(8,128)(2,1)} %copy.86), calls=%async_computation.2 | async-start | bytes 4194304 | tf_op jit(solution)/shard_map/all_to_all | solution.py:104
  275.9 52.1 %all-to-all-done.1 = bf16[128,6,1024]{2,1,0:T(8,128)(2,1)} async-done(((bf16[128,6,1024]{2,1,0:T(8,128)(2,1)}), bf16[128,6,1024]{2,1,0:T(8,128)(2,1)}, u32[]{:S(2)}, u32[]{:S(2)}) %all-to-all-start.1) | async-done | bytes 1572896 | tf_op jit(solution)/shard_map/all_to_all | solution.py:104
  328.0 2.5 copy.88
  330.4 7.9 %gather_fusion.1 = bf16[512,1024]{1,0:T(8,128)(2,1)} fusion(bf16[128,6,1024]{2,0,1:T(8,128)(2,1)S(1)} %copy.88, s32[512]{0:T(512)S(1)} %reshape.74), kind=kCustom, calls=%fused_computation.1 | custom fusion | bytes 2101248 | tf_op jit(solution)/shard_map/gather | solution.py:105
  338.3 1.9 fusion.6
  340.2 1.6 add_convert_fusion
  (52 shorter events, 1.7 us)
Async XLA Ops:
  6.5 236.2 %copy-start = (bf16[1,384,2048]{2,1,0:T(8,128)(2,1)S(1)}, bf16[1,384,2048]{2,1,0:T(8,128)(2,1)}, u32[]{:S(2)}) copy-start(bf16[1,384,2048]{2,1,0:T(8,128)(2,1)} %param.25) | copy-start | bytes 4718596
  6.5 90.8 %all-gather.3.cloned.1.call-start = ((), (), s32[]{:S(2)}) async-start(), calls=%async_computation.3 | async-start | bytes 10485760 | tf_op jit(solution)/shard_map/all_gather | solution.py:66
  7.3 3.0 copy-start.4
  7.3 250.4 %reduce-scatter.2.cloned.1.call-start = ((), (), s32[]{:S(2)}) async-start(), calls=%async_computation.4 | async-start | bytes 4718592 | tf_op jit(solution)/shard_map/reduce_scatter | solution.py:101
  10.3 2.8 copy-start.5
  10.3 2.8 copy-start.6
  13.3 4.7 %copy-start.2 = (bf16[2048,2,128]{2,0,1:T(8,128)(2,1)S(1)}, bf16[2048,2,128]{2,0,1:T(8,128)(2,1)}, u32[]{:S(2)}) copy-start(bf16[2048,2,128]{2,0,1:T(8,128)(2,1)} %copy.75) | copy-start | bytes 3145732
  17.9 5.1 %copy-start.7 = (s32[64,8]{0,1:T(8,128)S(1)}, s32[64,8]{0,1:T(8,128)}, u32[]{:S(2)}) copy-start(s32[64,8]{0,1:T(8,128)} %param.21) | copy-start | bytes 6148
  97.4 7.5 %copy-start.3 = (bf16[64,2048]{1,0:T(8,128)(2,1)S(1)}, bf16[64,2048]{1,0:T(8,128)(2,1)}, u32[]{:S(2)}) copy-start(bf16[64,2048]{1,0:T(8,128)(2,1)} %param.19) | copy-start | bytes 786436
  102.4 3.5 %copy-start.8 = (f32[2048]{0:T(1024)S(1)}, f32[2048]{0:T(1024)}, u32[]{:S(2)}) copy-start(f32[2048]{0:T(1024)} %param.20) | copy-start | bytes 24580
  236.4 4.3 %copy-start.1 = (bf16[768,2048]{1,0:T(8,128)(2,1)S(1)}, bf16[768,2048]{1,0:T(8,128)(2,1)}, u32[]{:S(2)}) copy-start(bf16[768,2048]{1,0:T(8,128)(2,1)} %reshape.65) | copy-start | bytes 9437188
  236.4 4.3 %copy-start.10 = (bf16[1,2048,384]{2,1,0:T(8,128)(2,1)S(1)}, bf16[1,2048,384]{2,1,0:T(8,128)(2,1)}, u32[]{:S(2)}) copy-start(bf16[1,2048,384]{2,1,0:T(8,128)(2,1)} %param.24) | copy-start | bytes 4718596
  261.3 14.5 %copy-start.9 = (f32[64,8]{0,1:T(8,128)S(1)}, f32[64,8]{0,1:T(8,128)}, u32[]{:S(2)}) copy-start(f32[64,8]{0,1:T(8,128)} %param.22) | copy-start | bytes 6148
  261.3 66.6 %all-to-all-start.1 = ((bf16[128,6,1024]{2,1,0:T(8,128)(2,1)}), bf16[128,6,1024]{2,1,0:T(8,128)(2,1)}, u32[]{:S(2)}, u32[]{:S(2)}) async-start(bf16[128,6,1024]{2,1,0:T(8,128)(2,1)} %copy.86), calls=%async_computation.2 | async-start | bytes 4194304 | tf_op jit(solution)/shard_map/all_to_all | solution.py:104
Sparse Core Ops, SparseCore 0:
  9.1 88.1 all-gather.2
  246.4 11.2 reduce-scatter.1
